TPU v7x, 32 devices: a whole 2x2x4 slice. The times are simulated.
32 devices in a mesh: row: 8 (over y, x, core), col: 4 (over z).
Axes of the slice: x: 2, y: 2, z: 4, core: 2. Of those that a mesh axis runs over, the one named last changes fastest.
Arguments:
- tensor: float32 [128, 128, 768], P('row', 'col'), may hold values from -6 to 6
- start_one: float32 [128, 64], P('row'), may hold values from -0.5 to 0.5
- start_two: float32 [128, 64], P('col'), may hold values from -0.5 to 0.5
- start_three: float32 [768, 64], replicated, may hold values from -0.21875 to 0.21875
Outputs:
- factor_one: float32 [128, 64], replicated
- factor_two: float32 [128, 64], replicated
- factor_three: float32 [768, 64], replicated
- core: float32 [64, 64, 64], P(None, 'row', 'col')
All inputs are finite; a program needn't handle non-finite values.
Results may differ from a plain program's by a relative error of at most 0.0003.
Values sent between devices are 32-bit elements; how exact they have to be, the bound alone decides.
A program may use at most 64 MiB of HBM per device.

v0:
```python
import math
import jax
import jax.numpy as jnp
from jax import lax
from jax.sharding import PartitionSpec as P

STEPS = 4
HIGHEST = lax.Precision.HIGHEST


def product(left, right):
    return jnp.dot(left, right, precision=HIGHEST, preferred_element_type=jnp.float32)


def left_product(left, right):
    return lax.dot_general(
        left, right, (((0,), (0,)), ((), ())), precision=HIGHEST, preferred_element_type=jnp.float32
    )


def right_product(left, right):
    return lax.dot_general(
        left, right, (((1,), (1,)), ((), ())), precision=HIGHEST, preferred_element_type=jnp.float32
    )


def cross_product(left, right):
    return lax.dot_general(
        left, right, (((0,), (1,)), ((), ())), precision=HIGHEST, preferred_element_type=jnp.float32
    )


def orthonormal(matrix, inner):
    lower = jnp.linalg.cholesky(inner)
    return jax.scipy.linalg.solve_triangular(lower, matrix.T, lower=True).T


def pairing(local, block_rows):
    return right_product(local, block_rows)


def settle(gram_whole, basis):
    for iteration in range(STEPS):
        image = product(gram_whole, basis)
        basis = orthonormal(image, left_product(image, image))
    return basis


def on_device(tensor, start_one, start_two, start_three):
    rows_one, rows_two, depth = tensor.shape
    rank = start_three.shape[1]
    flat = tensor.reshape(rows_one * rows_two, depth)
    contracted = cross_product(start_three, flat).reshape(rank, rows_one, rows_two)
    part_one = jnp.einsum("cij,jb->ibc", contracted, start_two, precision=HIGHEST).reshape(
        rows_one, rank * rank
    )
    slab_one = lax.psum_scatter(part_one, "col", scatter_dimension=1, tiled=True)
    slab_rows_one = lax.all_gather(slab_one, "row", axis=0, tiled=True)
    gram_one = lax.psum(right_product(slab_rows_one, slab_rows_one), "col")
    basis_one = settle(gram_one, lax.all_gather(start_one, "row", axis=0, tiled=True))
    own_one = lax.dynamic_slice_in_dim(basis_one, lax.axis_index("row") * rows_one, rows_one, 0)
    part_two = jnp.einsum("cij,ia->jac", contracted, own_one, precision=HIGHEST).reshape(
        rows_two, rank * rank
    )
    slab_two = lax.psum_scatter(part_two, "row", scatter_dimension=1, tiled=True)
    slab_rows_two = lax.all_gather(slab_two, "col", axis=0, tiled=True)
    gram_two = lax.psum(right_product(slab_rows_two, slab_rows_two), "row")
    basis_two = settle(gram_two, lax.all_gather(start_two, "col", axis=0, tiled=True))
    own_two = lax.dynamic_slice_in_dim(basis_two, lax.axis_index("col") * rows_two, rows_two, 0)
    received = lax.all_to_all(tensor, "row", split_axis=2, concat_axis=0, tiled=True)
    count, items, cells = received.shape
    merged = left_product(basis_one, received.reshape(count, items * cells))
    mixed = merged.reshape(rank, items, cells)
    part_three = jnp.einsum("ajk,jb->kba", mixed, own_two, precision=HIGHEST)
    cells_here = part_three.shape[0]
    slab_three = lax.psum_scatter(
        part_three.reshape(cells_here, rank * rank), "col", scatter_dimension=1, tiled=True
    )
    gram_part_three = pairing(slab_three, lax.all_gather(slab_three, "row", axis=0, tiled=True))
    gram_three = lax.psum(gram_part_three, "col")
    basis_three = start_three
    own_three = start_three
    for iteration in range(STEPS):
        image = product(gram_three, basis_three)
        inner = lax.psum(left_product(image, image), "row")
        own_three = orthonormal(image, inner)
        basis_three = lax.all_gather(own_three, "row", axis=0, tiled=True)
    core_part = left_product(own_three, slab_three)
    core_part = core_part.reshape(rank, core_part.shape[1] // rank, rank)
    core = lax.psum_scatter(core_part, "row", scatter_dimension=2, tiled=True).transpose(0, 2, 1)
    factor_one = basis_one * math.sqrt(basis_one.shape[0])
    factor_two = basis_two * math.sqrt(basis_two.shape[0])
    factor_three = basis_three * math.sqrt(basis_three.shape[0])
    return (factor_one, factor_two, factor_three, core)


def solution(mesh):
    return jax.shard_map(
        on_device,
        mesh=mesh,
        in_specs=(P("row", "col", None), P("row", None), P("col", None), P()),
        out_specs=(P(), P(), P(), P(None, "row", "col")),
        check_vma=False,
    )
```

profile of v0, /device:TPU:0, one launch (start us, length us, event | category | flops | bytes accessed | tf_op | source)
XLA Modules:
  0.0 638.1 jit_solution(973068163309146630)
XLA Ops:
  13.1 22.8 %reduce-scatter.5.cloned.1.call-done = f32[16,1024]{1,0:T(8,128)} async-done(((f32[16,4096]{1,0:T(8,128)}), f32[16,1024]{1,0:T(8,128)}) %reduce-scatter.5.cloned.1.call-update) | async-done | bytes 65552 | tf_op jit(solution)/shard_map/reduce_scatter | solution.py:57
  35.9 10.1 %all_gather.27 = f32[128,1024]{1,0:T(8,128)S(1)} all-gather(f32[16,1024]{1,0:T(8,128)} %reduce-scatter.5.cloned.1.call-done), channel_id=1, replica_groups=mesh['row'=8,'col'=4] {'row'}, dimensions={0}, use_global_device_ids=true | all-gather | bytes 589824 | tf_op jit(solution)/shard_map/all_gather | solution.py:58
  47.2 5.0 copy.67
  52.3 7.6 %reshape.61 = f32[8,1,49152]{2,1,0:T(1,128)} reshape(f32[768,16,32]{2,1,0:T(8,128)} %bitcast.262) | data formatting | bytes 3145728
  63.7 24.3 %all_gather.28 = f32[128,64]{1,0:T(8,128)S(1)} all-gather(f32[16,64]{1,0:T(8,128)S(1)} %copy-done.7), channel_id=1, replica_groups=mesh['row'=8,'col'=4] {'row'}, dimensions={0}, use_global_device_ids=true | all-gather | bytes 36864 | tf_op jit(solution)/shard_map/all_gather | solution.py:60
  89.5 5.8 cholesky.194
  96.7 4.9 custom-call.18
  103.2 5.8 cholesky.205
  110.4 4.9 custom-call.19
  116.9 5.8 cholesky.216
  124.1 4.9 custom-call.20
  129.8 5.8 cholesky.227
  137.0 4.9 custom-call.21
  144.4 13.1 %all_gather.30 = f32[128,64]{1,0:T(8,128)S(1)} all-gather(f32[32,64]{1,0:T(8,128)S(1)} %copy-done.6), channel_id=1, replica_groups=mesh['row'=8,'col'=4] {'col'}, dimensions={0}, use_global_device_ids=true | all-gather | bytes 40960 | tf_op jit(solution)/shard_map/all_gather | solution.py:68
  157.6 18.4 %reduce-scatter.7.cloned.1.call-done = f32[32,512]{1,0:T(8,128)} async-done(((f32[32,4096]{1,0:T(8,128)}), f32[32,512]{1,0:T(8,128)}) %reduce-scatter.7.cloned.1.call-update) | async-done | bytes 65552 | tf_op jit(solution)/shard_map/reduce_scatter | solution.py:65
  176.0 14.0 %all_gather.29 = f32[128,512]{1,0:T(8,128)S(1)} all-gather(f32[32,512]{1,0:T(8,128)} %reduce-scatter.7.cloned.1.call-done), channel_id=1, replica_groups=mesh['row'=8,'col'=4] {'col'}, dimensions={0}, use_global_device_ids=true | all-gather | bytes 327680 | tf_op jit(solution)/shard_map/all_gather | solution.py:66
  196.2 4.7 reshape.62
  200.9 5.2 copy.68
  213.9 31.0 %all-reduce.6.cloned.1.call-done = f32[128,128]{1,0:T(8,128)} async-done(((f32[128,128]{1,0:T(8,128)}), f32[128,128]{1,0:T(8,128)}) %all-reduce.6.cloned.1.call-update) | async-done | bytes 65552 | tf_op jit(solution)/shard_map/psum | solution.py:67
  246.4 5.8 cholesky.238
  253.6 4.9 custom-call.22
  260.1 5.8 cholesky.249
  267.3 4.9 custom-call.23
  273.9 5.8 cholesky.260
  281.0 4.9 custom-call.24
  286.7 5.8 cholesky.271
  293.9 5.0 custom-call.25
  304.2 43.1 %reduce-scatter.9.cloned.1.call-done = f32[96,1024]{0,1:T(8,128)} async-done(((f32[96,4096]{0,1:T(8,128)}), f32[96,1024]{0,1:T(8,128)}) %reduce-scatter.9.cloned.1.call-update) | async-done | bytes 393232 | tf_op jit(solution)/shard_map/reduce_scatter | solution.py:76
  349.4 31.5 %all-gather.6.cloned.1.call-done = f32[768,1024]{1,0:T(8,128)} async-done(((f32[96,1024]{1,0:T(8,128)}), f32[768,1024]{1,0:T(8,128)}) %all-gather.6.cloned.1.call-update) | async-done | bytes 3145744 | tf_op jit(solution)/shard_map/all_gather | solution.py:79
  380.9 5.3 fusion.94
  386.9 35.4 %all-reduce.8.cloned.1.call-done = f32[96,768]{1,0:T(8,128)} async-done(((f32[96,768]{1,0:T(8,128)}), f32[96,768]{1,0:T(8,128)}) %all-reduce.8.cloned.1.call-update) | async-done | bytes 294928 | tf_op jit(solution)/shard_map/psum | solution.py:80
  424.0 22.4 %psum.52 = f32[64,64]{0,1:T(8,128)S(1)} all-reduce(f32[64,64]{0,1:T(8,128)S(1)} %fusion.96), channel_id=1, replica_groups=mesh['row'=8,'col'=4] {'row'}, use_global_device_ids=true, to_apply=%region_8.11 | all-reduce | flops 4096 | bytes 32768 | tf_op jit(solution)/shard_map/psum | solution.py:85
  446.4 5.8 cholesky.282
  453.6 4.9 custom-call.26
  458.8 9.3 %all-gather = f32[8,96,64]{1,2,0:T(8,128)S(1)} all-gather(f32[1,96,64]{1,2,0:T(8,128)S(1)} %convolution_bitcast_fusion.5), channel_id=1, replica_groups=mesh['row'=8,'col'=4] {'row'}, dimensions={0}, use_global_device_ids=true | all-gather | bytes 221184 | tf_op jit(solution)/shard_map/all_gather | solution.py:87
  469.0 23.9 %psum.53 = f32[64,64]{0,1:T(8,128)S(1)} all-reduce(f32[64,64]{0,1:T(8,128)S(1)} %fusion.98), channel_id=1, replica_groups=mesh['row'=8,'col'=4] {'row'}, use_global_device_ids=true, to_apply=%region_9.0 | all-reduce | flops 4096 | bytes 32768 | tf_op jit(solution)/shard_map/psum | solution.py:85
  493.0 5.8 cholesky.293
  500.2 4.9 custom-call.27
  505.3 8.3 %all-gather.1 = f32[8,96,64]{1,2,0:T(8,128)S(1)} all-gather(f32[1,96,64]{1,2,0:T(8,128)S(1)} %convolution_bitcast_fusion.4), channel_id=1, replica_groups=mesh['row'=8,'col'=4] {'row'}, dimensions={0}, use_global_device_ids=true | all-gather | bytes 221184 | tf_op jit(solution)/shard_map/all_gather | solution.py:87
  514.6 23.6 %psum.54 = f32[64,64]{0,1:T(8,128)S(1)} all-reduce(f32[64,64]{0,1:T(8,128)S(1)} %fusion.100), channel_id=1, replica_groups=mesh['row'=8,'col'=4] {'row'}, use_global_device_ids=true, to_apply=%region_10.0 | all-reduce | flops 4096 | bytes 32768 | tf_op jit(solution)/shard_map/psum | solution.py:85
  538.3 5.8 cholesky.304
  545.5 4.9 custom-call.28
  550.6 9.3 %all-gather.2 = f32[8,96,64]{1,2,0:T(8,128)S(1)} all-gather(f32[1,96,64]{1,2,0:T(8,128)S(1)} %convolution_bitcast_fusion.3), channel_id=1, replica_groups=mesh['row'=8,'col'=4] {'row'}, dimensions={0}, use_global_device_ids=true | all-gather | bytes 221184 | tf_op jit(solution)/shard_map/all_gather | solution.py:87
  560.8 23.6 %psum.55 = f32[64,64]{0,1:T(8,128)S(1)} all-reduce(f32[64,64]{0,1:T(8,128)S(1)} %fusion.102), channel_id=1, replica_groups=mesh['row'=8,'col'=4] {'row'}, use_global_device_ids=true, to_apply=%region_11.15 | all-reduce | flops 4096 | bytes 32768 | tf_op jit(solution)/shard_map/psum | solution.py:85
  584.5 5.8 cholesky.315
  591.7 4.9 custom-call.29
  599.4 8.3 %all-gather.3 = f32[8,96,64]{1,2,0:T(8,128)S(1)} all-gather(f32[1,96,64]{1,2,0:T(8,128)S(1)} %bitcast.267), channel_id=1, replica_groups=mesh['row'=8,'col'=4] {'row'}, dimensions={0}, use_global_device_ids=true | all-gather | bytes 221184 | tf_op jit(solution)/shard_map/all_gather | solution.py:87
  608.7 22.2 %reduce-scatter.11.cloned.1.call-done = f32[64,16,8]{0,1,2:T(8,128)} async-done(((f32[64,16,64]{0,1,2:T(8,128)}), f32[64,16,8]{0,1,2:T(8,128)}) %reduce-scatter.11.cloned.1.call-update) | async-done | bytes 32784 | tf_op jit(solution)/shard_map/reduce_scatter | solution.py:90
  (161 shorter events, 71.1 us)
Async XLA Ops:
  7.2 0.9 copy-start
  7.2 3.7 copy-start.6
  7.2 28.7 %reduce-scatter.5.cloned.1.call-start = ((), (), s32[]{:S(2)}) async-start(), calls=%async_computation.5 | async-start | bytes 327680 | tf_op jit(solution)/shard_map/reduce_scatter | solution.py:57
  12.1 35.1 %copy-start.1 = (f32[16,32,768]{2,1,0:T(8,128)S(1)}, f32[16,32,768]{2,1,0:T(8,128)}, u32[]{:S(2)}) copy-start(f32[16,32,768]{2,1,0:T(8,128)} %param.9) | copy-start | bytes 4718596
  13.0 75.0 %all-reduce.4.cloned.1.call-start = ((), (), s32[]{:S(2)}) async-start(), calls=%async_computation.6 | async-start | bytes 131072 | tf_op jit(solution)/shard_map/psum | solution.py:59
  59.9 3.8 copy-start.7
  59.9 131.4 %all-to-all-start = ((f32[8,1,49152]{2,1,0:T(1,128)}), f32[8,1,49152]{2,1,0:T(1,128)S(1)}, u32[]{:S(2)}, u32[]{:S(2)}) async-start(f32[8,1,49152]{2,1,0:T(1,128)} %reshape.61), calls=%async_computation.2 | async-start | bytes 3145728 | tf_op jit(solution)/shard_map/all_to_all | solution.py:70
  63.6 112.3 %reduce-scatter.7.cloned.1.call-start = ((), (), s32[]{:S(2)}) async-start(), calls=%async_computation.7 | async-start | bytes 589824 | tf_op jit(solution)/shard_map/reduce_scatter | solution.py:65
  88.0 41.2 %copy-start.4 = (f32[128,128]{1,0:T(8,128)S(1)}, f32[128,128]{1,0:T(8,128)}, u32[]{:S(2)}) copy-start(f32[128,128]{1,0:T(8,128)} %all-reduce.4.cloned.1.call-done) | copy-start | bytes 196612
  144.4 100.6 %all-reduce.6.cloned.1.call-start = ((), (), s32[]{:S(2)}) async-start(), calls=%async_computation.8 | async-start | bytes 131072 | tf_op jit(solution)/shard_map/psum | solution.py:67
  191.0 156.3 %reduce-scatter.9.cloned.1.call-start = ((), (), s32[]{:S(2)}) async-start(), calls=%async_computation.9 | async-start | bytes 2621440 | tf_op jit(solution)/shard_map/reduce_scatter | solution.py:76
  245.0 41.2 %copy-start.5 = (f32[128,128]{1,0:T(8,128)S(1)}, f32[128,128]{1,0:T(8,128)}, u32[]{:S(2)}) copy-start(f32[128,128]{1,0:T(8,128)} %all-reduce.6.cloned.1.call-done) | copy-start | bytes 196612
  304.1 76.8 %all-gather.6.cloned.1.call-start = ((), (), s32[]{:S(2)}) async-start(), calls=%async_computation.10 | async-start | bytes 3538944 | tf_op jit(solution)/shard_map/all_gather | solution.py:79
  347.3 33.6 %copy-start.2 = (f32[96,1024]{0,1:T(8,128)S(1)}, f32[96,1024]{0,1:T(8,128)}, u32[]{:S(2)}) copy-start(f32[96,1024]{0,1:T(8,128)} %reduce-scatter.9.cloned.1.call-done) | copy-start | bytes 1179652
  349.4 72.9 %all-reduce.8.cloned.1.call-start = ((), (), s32[]{:S(2)}) async-start(), calls=%async_computation.11 | async-start | bytes 589824 | tf_op jit(solution)/shard_map/psum | solution.py:80
  386.2 244.8 %reduce-scatter.11.cloned.1.call-start = ((), (), s32[]{:S(2)}) async-start(), calls=%async_computation.12 | async-start | bytes 589824 | tf_op jit(solution)/shard_map/reduce_scatter | solution.py:90
  422.3 46.0 %copy-start.3 = (f32[96,768]{1,0:T(8,128)S(1)}, f32[96,768]{1,0:T(8,128)}, u32[]{:S(2)}) copy-start(f32[96,768]{1,0:T(8,128)} %all-reduce.8.cloned.1.call-done) | copy-start | bytes 884740
Sparse Core Ops, SparseCore 0:
  13.2 22.7 reduce-scatter.4
  47.4 31.5 all-reduce.3
  144.5 31.4 reduce-scatter.6
  191.2 53.7 all-reduce.5
  304.3 43.0 reduce-scatter.8
  349.5 31.3 all-gather.5
  386.4 35.9 all-reduce.7
  598.9 32.0 reduce-scatter.10
where the time goes:
time: 644 us; the launch traced here: 638 us
  waiting for transfers between devices  205 us (32%)
  blocking collectives  190 us (30%)
  other arithmetic  151 us (23%)
  local copies, waits for them, and re-layouts  39.1 us (6%)
  matrix products  33.9 us (5%)
  between operations  15.1 us (2%)
    psum x4, blocking collectives, on_device(): inner = lax.psum(left_product(image, image), 'row')  93.5 us
    another operation x36, other arithmetic, orthonormal(): lower = jnp.linalg.cholesky(inner)  78.2 us
    another operation x24, other arithmetic, orthonormal(): return jax.scipy.linalg.solve_triangular(lower, matrix.T, lower=True).T  66.7 us
    reduce_scatter x1, waiting for transfers between devices, on_device(): lax.psum_scatter(part_three.reshape(cells_here, rank * rank), 'col', scat...  43.1 us
    psum x1, waiting for transfers between devices, on_device(): gram_three = lax.psum(gram_part_three, 'col')  35.4 us
    all_gather x4, blocking collectives, on_device(): basis_three = lax.all_gather(own_three, 'row', axis=0, tiled=True)  35.2 us
    all_gather x1, waiting for transfers between devices, on_device(): lax.all_gather(slab_three, 'row', axis=0, tiled=True)  31.5 us
    psum x1, waiting for transfers between devices, on_device(): gram_two = lax.psum(right_product(slab_rows_two, slab_rows_two), 'row')  31 us
  transfers between devices with their start and end apart: 9, of which 7 were waited for; matrix products, arithmetic and copies ran while one was open for 15% of the time, Pallas kernels for 0%

commit v1 on v0

--- a/solution.py
+++ b/solution.py
@@ -82,7 +82,7 @@
     own_three = start_three
     for iteration in range(STEPS):
         image = product(gram_three, basis_three)
-        inner = lax.psum(left_product(image, image), "row")
+        inner = jnp.sum(lax.all_gather(left_product(image, image), "row"), axis=0)
         own_three = orthonormal(image, inner)
         basis_three = lax.all_gather(own_three, "row", axis=0, tiled=True)
     core_part = left_product(own_three, slab_three)

time: 644 us -> 587 us (0.911)
  blocking collectives: 190 us -> 133 us
    psum x4 -> x0, blocking collectives: 93.5 us -> none  [on_device(): inner = lax.psum(left_product(image, image), 'row')]
    all_gather x0 -> x4, blocking collectives: none -> 34.5 us  [on_device(): inner = jnp.sum(lax.all_gather(left_product(image, image), 'row'), axis=0)]
  transfers between devices with their start and end apart: 9 -> 9, of which waited for: 7 -> 7; matrix products, arithmetic and copies ran while one was open for 15% -> 16% of each run, Pallas kernels for 0% -> 0%
where the time goes in v1:
time: 587 us; the launch traced here: 581 us
  waiting for transfers between devices  205 us (35%)
  other arithmetic  151 us (26%)
  blocking collectives  133 us (23%)
  local copies, waits for them, and re-layouts  39 us (7%)
  matrix products  33.9 us (6%)
  between operations  15.1 us (3%)
    another operation x36, other arithmetic, orthonormal(): lower = jnp.linalg.cholesky(inner)  78.2 us
    another operation x24, other arithmetic, orthonormal(): return jax.scipy.linalg.solve_triangular(lower, matrix.T, lower=True).T  66.7 us
    reduce_scatter x1, waiting for transfers between devices, on_device(): lax.psum_scatter(part_three.reshape(cells_here, rank * rank), 'col', scat...  43.1 us
    all_gather x4, blocking collectives, on_device(): basis_three = lax.all_gather(own_three, 'row', axis=0, tiled=True)  37 us
    psum x1, waiting for transfers between devices, on_device(): gram_three = lax.psum(gram_part_three, 'col')  35.4 us
    all_gather x4, blocking collectives, on_device(): inner = jnp.sum(lax.all_gather(left_product(image, image), 'row'), axis=0)  34.5 us
    all_gather x1, waiting for transfers between devices, on_device(): lax.all_gather(slab_three, 'row', axis=0, tiled=True)  31.5 us
    psum x1, waiting for transfers between devices, on_device(): gram_two = lax.psum(right_product(slab_rows_two, slab_rows_two), 'row')  31 us
  transfers between devices with their start and end apart: 9, of which 7 were waited for; matrix products, arithmetic and copies ran while one was open for 16% of the time, Pallas kernels for 0%

profile of v1, /device:TPU:0, one launch (start us, length us, event | category | flops | bytes accessed | tf_op | source)
XLA Modules:
  0.0 581.0 jit_solution(2219288831843532793)
XLA Ops:
  13.1 22.8 %reduce-scatter.5.cloned.1.call-done = f32[16,1024]{1,0:T(8,128)} async-done(((f32[16,4096]{1,0:T(8,128)}), f32[16,1024]{1,0:T(8,128)}) %reduce-scatter.5.cloned.1.call-update) | async-done | bytes 65552 | tf_op jit(solution)/shard_map/reduce_scatter | solution.py:57
  35.9 10.1 %all_gather.51 = f32[128,1024]{1,0:T(8,128)S(1)} all-gather(f32[16,1024]{1,0:T(8,128)} %reduce-scatter.5.cloned.1.call-done), channel_id=1, replica_groups=mesh['row'=8,'col'=4] {'row'}, dimensions={0}, use_global_device_ids=true | all-gather | bytes 589824 | tf_op jit(solution)/shard_map/all_gather | solution.py:58
  47.2 5.0 copy.59
  52.3 7.6 %reshape.65 = f32[8,1,49152]{2,1,0:T(1,128)} reshape(f32[768,16,32]{2,1,0:T(8,128)} %bitcast.266) | data formatting | bytes 3145728
  63.7 24.3 %all_gather.52 = f32[128,64]{1,0:T(8,128)S(1)} all-gather(f32[16,64]{1,0:T(8,128)S(1)} %copy-done.7), channel_id=1, replica_groups=mesh['row'=8,'col'=4] {'row'}, dimensions={0}, use_global_device_ids=true | all-gather | bytes 36864 | tf_op jit(solution)/shard_map/all_gather | solution.py:60
  89.5 5.8 %cholesky.194 = f32[64,64]{1,0:T(8,128)S(1)} custom-call(f32[64,64]{1,0:T(8,128)S(1)} %fusion.64), custom_call_target="Cholesky" | custom-call | tf_op jit(solution)/shard_map/jit(cholesky)/cholesky | solution.py:34
  96.7 4.9 custom-call.18
  103.2 5.8 %cholesky.205 = f32[64,64]{1,0:T(8,128)S(1)} custom-call(f32[64,64]{1,0:T(8,128)S(1)} %fusion.60), custom_call_target="Cholesky" | custom-call | tf_op jit(solution)/shard_map/jit(cholesky)/cholesky | solution.py:34
  110.4 4.9 custom-call.19
  116.9 5.8 %cholesky.216 = f32[64,64]{1,0:T(8,128)S(1)} custom-call(f32[64,64]{1,0:T(8,128)S(1)} %fusion.56), custom_call_target="Cholesky" | custom-call | tf_op jit(solution)/shard_map/jit(cholesky)/cholesky | solution.py:34
  124.1 4.9 custom-call.20
  129.8 5.8 %cholesky.227 = f32[64,64]{1,0:T(8,128)S(1)} custom-call(f32[64,64]{1,0:T(8,128)S(1)} %fusion.52), custom_call_target="Cholesky" | custom-call | tf_op jit(solution)/shard_map/jit(cholesky)/cholesky | solution.py:34
  137.0 4.9 custom-call.21
  144.4 13.1 %all_gather.54 = f32[128,64]{1,0:T(8,128)S(1)} all-gather(f32[32,64]{1,0:T(8,128)S(1)} %copy-done.6), channel_id=1, replica_groups=mesh['row'=8,'col'=4] {'col'}, dimensions={0}, use_global_device_ids=true | all-gather | bytes 40960 | tf_op jit(solution)/shard_map/all_gather | solution.py:68
  157.6 18.4 %reduce-scatter.7.cloned.1.call-done = f32[32,512]{1,0:T(8,128)} async-done(((f32[32,4096]{1,0:T(8,128)}), f32[32,512]{1,0:T(8,128)}) %reduce-scatter.7.cloned.1.call-update) | async-done | bytes 65552 | tf_op jit(solution)/shard_map/reduce_scatter | solution.py:65
  176.0 14.0 %all_gather.53 = f32[128,512]{1,0:T(8,128)S(1)} all-gather(f32[32,512]{1,0:T(8,128)} %reduce-scatter.7.cloned.1.call-done), channel_id=1, replica_groups=mesh['row'=8,'col'=4] {'col'}, dimensions={0}, use_global_device_ids=true | all-gather | bytes 327680 | tf_op jit(solution)/shard_map/all_gather | solution.py:66
  196.2 4.7 reshape.66
  200.9 5.2 copy.60
  213.9 31.0 %all-reduce.6.cloned.1.call-done = f32[128,128]{1,0:T(8,128)} async-done(((f32[128,128]{1,0:T(8,128)}), f32[128,128]{1,0:T(8,128)}) %all-reduce.6.cloned.1.call-update) | async-done | bytes 65552 | tf_op jit(solution)/shard_map/psum | solution.py:67
  246.4 5.8 %cholesky.238 = f32[64,64]{1,0:T(8,128)S(1)} custom-call(f32[64,64]{1,0:T(8,128)S(1)} %fusion.47), custom_call_target="Cholesky" | custom-call | tf_op jit(solution)/shard_map/jit(cholesky)/cholesky | solution.py:34
  253.6 4.9 custom-call.22
  260.1 5.8 %cholesky.249 = f32[64,64]{1,0:T(8,128)S(1)} custom-call(f32[64,64]{1,0:T(8,128)S(1)} %fusion.43), custom_call_target="Cholesky" | custom-call | tf_op jit(solution)/shard_map/jit(cholesky)/cholesky | solution.py:34
  267.3 4.9 custom-call.23
  273.9 5.8 %cholesky.260 = f32[64,64]{1,0:T(8,128)S(1)} custom-call(f32[64,64]{1,0:T(8,128)S(1)} %fusion.39), custom_call_target="Cholesky" | custom-call | tf_op jit(solution)/shard_map/jit(cholesky)/cholesky | solution.py:34
  281.0 4.9 custom-call.24
  286.7 5.8 %cholesky.271 = f32[64,64]{1,0:T(8,128)S(1)} custom-call(f32[64,64]{1,0:T(8,128)S(1)} %fusion.35), custom_call_target="Cholesky" | custom-call | tf_op jit(solution)/shard_map/jit(cholesky)/cholesky | solution.py:34
  293.9 5.0 custom-call.25
  304.2 43.1 %reduce-scatter.9.cloned.1.call-done = f32[96,1024]{0,1:T(8,128)} async-done(((f32[96,4096]{0,1:T(8,128)}), f32[96,1024]{0,1:T(8,128)}) %reduce-scatter.9.cloned.1.call-update) | async-done | bytes 393232 | tf_op jit(solution)/shard_map/reduce_scatter | solution.py:76
  349.4 31.5 %all-gather.10.cloned.1.call-done = f32[768,1024]{1,0:T(8,128)} async-done(((f32[96,1024]{1,0:T(8,128)}), f32[768,1024]{1,0:T(8,128)}) %all-gather.10.cloned.1.call-update) | async-done | bytes 3145744 | tf_op jit(solution)/shard_map/all_gather | solution.py:79
  380.9 5.3 fusion.94
  386.9 35.4 %all-reduce.8.cloned.1.call-done = f32[96,768]{1,0:T(8,128)} async-done(((f32[96,768]{1,0:T(8,128)}), f32[96,768]{1,0:T(8,128)}) %all-reduce.8.cloned.1.call-update) | async-done | bytes 294928 | tf_op jit(solution)/shard_map/psum | solution.py:80
  424.0 9.3 %all-gather = f32[512,64]{1,0:T(8,128)S(1)} all-gather(f32[64,64]{1,0:T(8,128)S(1)} %fusion.96), channel_id=2, replica_groups=mesh['row'=8,'col'=4] {'row'}, dimensions={0}, use_global_device_ids=true | all-gather | bytes 147456 | tf_op jit(solution)/shard_map/all_gather | solution.py:85
  433.4 5.8 %cholesky.282 = f32[64,64]{1,0:T(8,128)S(1)} custom-call(f32[64,64]{1,0:T(8,128)S(1)} %fusion.28), custom_call_target="Cholesky" | custom-call | tf_op jit(solution)/shard_map/jit(cholesky)/cholesky | solution.py:34
  440.6 4.9 custom-call.26
  445.7 9.3 %all-gather.4 = f32[8,96,64]{1,2,0:T(8,128)S(1)} all-gather(f32[1,96,64]{1,2,0:T(8,128)S(1)} %convolution_bitcast_fusion.5), channel_id=1, replica_groups=mesh['row'=8,'col'=4] {'row'}, dimensions={0}, use_global_device_ids=true | all-gather | bytes 221184 | tf_op jit(solution)/shard_map/all_gather | solution.py:87
  455.9 8.6 %all-gather.1 = f32[512,64]{1,0:T(8,128)S(1)} all-gather(f32[64,64]{1,0:T(8,128)S(1)} %fusion.98), channel_id=3, replica_groups=mesh['row'=8,'col'=4] {'row'}, dimensions={0}, use_global_device_ids=true | all-gather | bytes 147456 | tf_op jit(solution)/shard_map/all_gather | solution.py:85
  464.6 5.8 %cholesky.293 = f32[64,64]{1,0:T(8,128)S(1)} custom-call(f32[64,64]{1,0:T(8,128)S(1)} %fusion.25), custom_call_target="Cholesky" | custom-call | tf_op jit(solution)/shard_map/jit(cholesky)/cholesky | solution.py:34
  471.8 4.9 custom-call.27
  476.9 9.3 %all-gather.5 = f32[8,96,64]{1,2,0:T(8,128)S(1)} all-gather(f32[1,96,64]{1,2,0:T(8,128)S(1)} %convolution_bitcast_fusion.4), channel_id=1, replica_groups=mesh['row'=8,'col'=4] {'row'}, dimensions={0}, use_global_device_ids=true | all-gather | bytes 221184 | tf_op jit(solution)/shard_map/all_gather | solution.py:87
  487.1 8.4 %all-gather.2 = f32[512,64]{1,0:T(8,128)S(1)} all-gather(f32[64,64]{1,0:T(8,128)S(1)} %fusion.100), channel_id=4, replica_groups=mesh['row'=8,'col'=4] {'row'}, dimensions={0}, use_global_device_ids=true | all-gather | bytes 147456 | tf_op jit(solution)/shard_map/all_gather | solution.py:85
  495.6 5.8 %cholesky.304 = f32[64,64]{1,0:T(8,128)S(1)} custom-call(f32[64,64]{1,0:T(8,128)S(1)} %fusion.22), custom_call_target="Cholesky" | custom-call | tf_op jit(solution)/shard_map/jit(cholesky)/cholesky | solution.py:34
  502.8 4.9 custom-call.28
  507.9 9.3 %all-gather.6 = f32[8,96,64]{1,2,0:T(8,128)S(1)} all-gather(f32[1,96,64]{1,2,0:T(8,128)S(1)} %convolution_bitcast_fusion.3), channel_id=1, replica_groups=mesh['row'=8,'col'=4] {'row'}, dimensions={0}, use_global_device_ids=true | all-gather | bytes 221184 | tf_op jit(solution)/shard_map/all_gather | solution.py:87
  518.1 8.4 %all-gather.3 = f32[512,64]{1,0:T(8,128)S(1)} all-gather(f32[64,64]{1,0:T(8,128)S(1)} %fusion.102), channel_id=5, replica_groups=mesh['row'=8,'col'=4] {'row'}, dimensions={0}, use_global_device_ids=true | all-gather | bytes 147456 | tf_op jit(solution)/shard_map/all_gather | solution.py:85
  526.6 5.8 %cholesky.315 = f32[64,64]{1,0:T(8,128)S(1)} custom-call(f32[64,64]{1,0:T(8,128)S(1)} %fusion.19), custom_call_target="Cholesky" | custom-call | tf_op jit(solution)/shard_map/jit(cholesky)/cholesky | solution.py:34
  533.7 4.9 custom-call.29
  541.5 9.2 %all-gather.7 = f32[8,96,64]{1,2,0:T(8,128)S(1)} all-gather(f32[1,96,64]{1,2,0:T(8,128)S(1)} %bitcast.275), channel_id=1, replica_groups=mesh['row'=8,'col'=4] {'row'}, dimensions={0}, use_global_device_ids=true | all-gather | bytes 221184 | tf_op jit(solution)/shard_map/all_gather | solution.py:87
  551.7 22.3 %reduce-scatter.11.cloned.1.call-done = f32[64,16,8]{0,1,2:T(8,128)} async-done(((f32[64,16,64]{0,1,2:T(8,128)}), f32[64,16,8]{0,1,2:T(8,128)}) %reduce-scatter.11.cloned.1.call-update) | async-done | bytes 32784 | tf_op jit(solution)/shard_map/reduce_scatter | solution.py:90
  (165 shorter events, 71.2 us)
Async XLA Ops:
  7.2 0.9 copy-start
  7.2 3.7 copy-start.6
  7.2 28.7 %reduce-scatter.5.cloned.1.call-start = ((), (), s32[]{:S(2)}) async-start(), calls=%async_computation.5 | async-start | bytes 327680 | tf_op jit(solution)/shard_map/reduce_scatter | solution.py:57
  12.1 35.1 %copy-start.1 = (f32[16,32,768]{2,1,0:T(8,128)S(1)}, f32[16,32,768]{2,1,0:T(8,128)}, u32[]{:S(2)}) copy-start(f32[16,32,768]{2,1,0:T(8,128)} %param.9) | copy-start | bytes 4718596
  13.0 75.0 %all-reduce.4.cloned.1.call-start = ((), (), s32[]{:S(2)}) async-start(), calls=%async_computation.6 | async-start | bytes 131072 | tf_op jit(solution)/shard_map/psum | solution.py:59
  59.9 3.8 copy-start.7
  59.9 131.4 %all-to-all-start = ((f32[8,1,49152]{2,1,0:T(1,128)}), f32[8,1,49152]{2,1,0:T(1,128)S(1)}, u32[]{:S(2)}, u32[]{:S(2)}) async-start(f32[8,1,49152]{2,1,0:T(1,128)} %reshape.65), calls=%async_computation.2 | async-start | bytes 3145728 | tf_op jit(solution)/shard_map/all_to_all | solution.py:70
  63.6 112.3 %reduce-scatter.7.cloned.1.call-start = ((), (), s32[]{:S(2)}) async-start(), calls=%async_computation.7 | async-start | bytes 589824 | tf_op jit(solution)/shard_map/reduce_scatter | solution.py:65
  88.0 41.2 %copy-start.4 = (f32[128,128]{1,0:T(8,128)S(1)}, f32[128,128]{1,0:T(8,128)}, u32[]{:S(2)}) copy-start(f32[128,128]{1,0:T(8,128)} %all-reduce.4.cloned.1.call-done) | copy-start | bytes 196612
  144.4 100.6 %all-reduce.6.cloned.1.call-start = ((), (), s32[]{:S(2)}) async-start(), calls=%async_computation.8 | async-start | bytes 131072 | tf_op jit(solution)/shard_map/psum | solution.py:67
  191.0 156.3 %reduce-scatter.9.cloned.1.call-start = ((), (), s32[]{:S(2)}) async-start(), calls=%async_computation.9 | async-start | bytes 2621440 | tf_op jit(solution)/shard_map/reduce_scatter | solution.py:76
  245.0 41.2 %copy-start.5 = (f32[128,128]{1,0:T(8,128)S(1)}, f32[128,128]{1,0:T(8,128)}, u32[]{:S(2)}) copy-start(f32[128,128]{1,0:T(8,128)} %all-reduce.6.cloned.1.call-done) | copy-start | bytes 196612
  304.1 76.8 %all-gather.10.cloned.1.call-start = ((), (), s32[]{:S(2)}) async-start(), calls=%async_computation.10 | async-start | bytes 3538944 | tf_op jit(solution)/shard_map/all_gather | solution.py:79
  347.3 33.6 %copy-start.2 = (f32[96,1024]{0,1:T(8,128)S(1)}, f32[96,1024]{0,1:T(8,128)}, u32[]{:S(2)}) copy-start(f32[96,1024]{0,1:T(8,128)} %reduce-scatter.9.cloned.1.call-done) | copy-start | bytes 1179652
  349.4 72.9 %all-reduce.8.cloned.1.call-start = ((), (), s32[]{:S(2)}) async-start(), calls=%async_computation.11 | async-start | bytes 589824 | tf_op jit(solution)/shard_map/psum | solution.py:80
  386.2 187.7 %reduce-scatter.11.cloned.1.call-start = ((), (), s32[]{:S(2)}) async-start(), calls=%async_computation.12 | async-start | bytes 589824 | tf_op jit(solution)/shard_map/reduce_scatter | solution.py:90
  422.3 32.9 %copy-start.3 = (f32[96,768]{1,0:T(8,128)S(1)}, f32[96,768]{1,0:T(8,128)}, u32[]{:S(2)}) copy-start(f32[96,768]{1,0:T(8,128)} %all-reduce.8.cloned.1.call-done) | copy-start | bytes 884740
Sparse Core Ops, SparseCore 0:
  13.2 22.7 reduce-scatter.4
  47.4 31.5 all-reduce.3
  144.5 31.4 reduce-scatter.6
  191.2 53.7 all-reduce.5
  304.3 43.0 reduce-scatter.8
  349.5 31.3 all-gather.9
  386.4 35.9 all-reduce.7
  541.0 32.9 reduce-scatter.10
